TPU v7x, 128 devices: a whole 4x4x4 slice. The times are simulated.
128 devices in a mesh: seq: 8 (over x, core), exp: 16 (over y, z).
Axes of the slice: x: 4, y: 4, z: 4, core: 2. Of those that a mesh axis runs over, the one named last changes fastest.
Arguments:
- xin: bfloat16 [512, 4, 8192], P('seq', None, 'exp'), may hold values from -6 to 6
- zin: bfloat16 [512, 4, 8192], P('seq', None, 'exp'), may hold values from -6 to 6
- conv_weight: float32 [4, 8192], P(None, 'exp'), may hold values from -3 to 3
- conv_bias: float32 [8192], P('exp'), may hold values from -3 to 3
- xproj_weight: bfloat16 [8192, 288], P('exp'), may hold values from -0.0625 to 0.0625
- dtproj_weight: bfloat16 [256, 8192], P(None, 'exp'), may hold values from -0.375 to 0.375
- dt_bias: float32 [8192], P('exp'), may hold values from -5 to -3
- a_log: float32 [16, 8192], P(None, 'exp'), may hold values from -3 to 1
- skip: float32 [8192], P('exp'), may hold values from 0.2 to 1
- out_weight: bfloat16 [8192, 4096], P('exp'), may hold values from -0.0625 to 0.0625
- resid: bfloat16 [512, 4, 4096], P(('seq', 'exp')), may hold values from -6 to 6
- norm_gain: float32 [4096], replicated, may hold values from 0.5 to 1.5
- expert_ids: int32 [512, 4, 2], P(('seq', 'exp')), may hold values from 0 to 7, all different within a row; in each aligned block of 16 rows (0 to 15, 16 to 31, ..., all dimensions but the last counted through in order) at most 8 rows name the same one
- gate_weights: bfloat16 [512, 4, 2], P(('seq', 'exp')), may hold values from 0.19921875 to 1
- w_gate: bfloat16 [16, 4096, 6144], P('exp', None, 'seq'), may hold values from -0.09375 to 0.09375
- w_up: bfloat16 [16, 4096, 6144], P('exp', None, 'seq'), may hold values from -0.09375 to 0.09375
- w_down: bfloat16 [16, 6144, 4096], P('exp', 'seq'), may hold values from -0.0546875 to 0.0546875
Outputs:
- layer_out: bfloat16 [512, 4, 4096], P(('seq', 'exp'))
Inputs may be any that keep to these rules, and one draw needn't show every extreme that they name: `expert_ids`: tokens are ordered by position, then document; in each aligned block of 16 such tokens (the tokens of one device), every expert is named at most 8 times, and in every draw some expert is named exactly 8 times in some block. Each token names 2 different experts.
All inputs are finite; a program needn't handle non-finite values.
Results may differ from a plain program's by a relative error of at most 0.03.
Values may be sent and summed in bfloat16 or wider, within the bound.
No kernel may reach another device: no remote copies, remote signals or barrier semaphores. Data moves between devices by JAX's collectives and lax.ppermute only.
A program may use at most 128 MiB of HBM per device.

v0:
```python
import jax
import jax.numpy as jnp
from jax import lax
from jax.sharding import PartitionSpec as P

D = 4096
STATE = 16
CONV = 4
RANK = 256
EXPERTS = 8
TOPK = 2


def passed_along(value, axis, by):
    count = lax.axis_size(axis)
    pairs = [(i, i + by) for i in range(count) if 0 <= i + by < count]
    return lax.ppermute(value, axis, pairs)


def entering(value, axis, join, neutral):
    place = lax.axis_index(axis)
    gathered = jax.tree.map(
        lambda a, kind: lax.all_gather(a.astype(kind), axis), value, (jnp.bfloat16, jnp.bfloat16)
    )
    state = jax.tree.map(lambda a, e: jnp.zeros_like(a) + jnp.asarray(e, a.dtype), value, neutral)

    def one(step, state):
        return join(
            state,
            jax.tree.map(
                lambda a, own: lax.dynamic_index_in_dim(a, step, 0, False).astype(own.dtype),
                gathered,
                value,
            ),
        )

    return lax.fori_loop(0, place, one, state)


def conv_inputs(window, conv_weight, conv_bias, length):
    running = jnp.zeros(window[:length].shape, jnp.float32) + conv_bias
    for offset in range(CONV):
        running = running + conv_weight[offset] * window[offset : offset + length]
    return running


def make_step(decay_rate):

    def advance(carry_state, series_now):
        step_now, input_now, read_now, value_now = series_now
        factor = jnp.exp(step_now[:, None, :] * decay_rate[None])
        carry_state = (
            factor * carry_state + (step_now * value_now)[:, None, :] * input_now[:, :, None]
        )
        return (carry_state, jnp.sum(read_now[:, :, None] * carry_state, axis=1))

    return advance


def chain(earlier, later):
    return (earlier[0] * later[0], later[0] * earlier[1] + later[1])


def slot_select(route_ids, capacity):
    flat_ids = route_ids.reshape(-1)
    onehot = (flat_ids[:, None] == jnp.arange(EXPERTS, dtype=jnp.int32)[None, :]).astype(jnp.int32)
    before = jnp.sum((jnp.cumsum(onehot, axis=0) - onehot) * onehot, axis=1)
    target = flat_ids * capacity + before
    matches = jnp.arange(EXPERTS * capacity, dtype=jnp.int32)[:, None] == target[None, :]
    return matches.reshape(EXPERTS * capacity, route_ids.shape[0], route_ids.shape[1])


def per_device(
    xin,
    zin,
    conv_weight,
    conv_bias,
    xproj_weight,
    dtproj_weight,
    dt_bias,
    a_log,
    skip,
    out_weight,
    resid,
    norm_gain,
    expert_ids,
    gate_weights,
    w_gate,
    w_up,
    w_down,
):
    section = xin.shape[0]
    edge_rows = passed_along(xin[section - (CONV - 1) :], "seq", 1)
    window = jnp.concatenate([edge_rows, xin], axis=0).astype(jnp.float32)
    inner_act = jax.nn.silu(conv_inputs(window, conv_weight, conv_bias, section)).astype(
        jnp.bfloat16
    )
    inner_f = inner_act.astype(jnp.float32)
    projected = jnp.einsum(
        "pbc,cr->pbr", inner_act, xproj_weight, preferred_element_type=jnp.float32
    )
    projected = lax.psum(projected.astype(jnp.bfloat16), "exp").astype(jnp.float32)
    low_rank = projected[..., :RANK].astype(jnp.bfloat16)
    in_state = projected[..., RANK : RANK + STATE]
    out_state = projected[..., RANK + STATE :]
    step_size = jax.nn.softplus(
        jnp.einsum("pbr,rc->pbc", low_rank, dtproj_weight, preferred_element_type=jnp.float32)
        + dt_bias
    )
    decay_rate = -jnp.exp(a_log)
    advance = make_step(decay_rate)
    series = (step_size, in_state, out_state, inner_f)
    zero_state = jnp.zeros((xin.shape[1], STATE, xin.shape[2]), jnp.float32)
    final_local, local_out = lax.scan(advance, zero_state, series)
    total_decay = jnp.exp(jnp.sum(step_size, axis=0)[:, None, :] * decay_rate[None])
    identity = (jnp.ones_like(total_decay), jnp.zeros_like(final_local))
    incoming = entering((total_decay, final_local), "seq", chain, identity)[1]
    ignored, ssm_out = lax.scan(advance, incoming, series)
    mixed_in = ((ssm_out + skip * inner_f) * jax.nn.silu(zin.astype(jnp.float32))).astype(
        jnp.bfloat16
    )
    row_block = mixed_in
    mamba_rows = lax.psum_scatter(
        jnp.einsum("pbc,cd->pbd", row_block, out_weight, preferred_element_type=jnp.float32).astype(
            jnp.bfloat16
        ),
        "exp",
        scatter_dimension=0,
        tiled=True,
    ).astype(jnp.float32)
    hidden_state = resid.astype(jnp.float32) + mamba_rows
    norm_scale = lax.rsqrt(jnp.mean(hidden_state * hidden_state, axis=-1, keepdims=True) + 1e-05)
    normed = (hidden_state * norm_scale * norm_gain).astype(jnp.bfloat16)
    row_count = resid.shape[0] * resid.shape[1]
    capacity = 2 * TOPK * row_count // EXPERTS
    splits = lax.axis_size("exp") // EXPERTS
    tokens = normed.reshape(row_count, D)
    route_ids = expert_ids.reshape(row_count, TOPK)
    gate_vals = gate_weights.reshape(row_count, TOPK)
    matches = slot_select(route_ids, capacity)
    chosen = jnp.sum(matches.astype(jnp.int32), axis=2).astype(jnp.bfloat16)
    outgoing = (
        jnp.dot(chosen, tokens, preferred_element_type=jnp.float32)
        .astype(jnp.bfloat16)
        .reshape(EXPERTS, capacity, D)
    )
    arrived = lax.all_to_all(
        jnp.tile(outgoing, (splits, 1, 1)), "exp", split_axis=0, concat_axis=0, tiled=True
    )
    everything = lax.all_gather(arrived, "seq", axis=0, tiled=True)
    row_block = everything
    expert_row_block = row_block.reshape(-1, D)
    gate_act = jnp.dot(expert_row_block, w_gate[0], preferred_element_type=jnp.float32)
    up_act = jnp.dot(expert_row_block, w_up[0], preferred_element_type=jnp.float32)
    hidden = (jax.nn.silu(gate_act) * up_act).astype(jnp.bfloat16)
    own_rows = lax.psum_scatter(
        jnp.dot(hidden, w_down[0], preferred_element_type=jnp.float32)
        .reshape(lax.axis_size("seq") * arrived.shape[0], capacity, D)
        .astype(jnp.bfloat16),
        "seq",
        scatter_dimension=0,
        tiled=True,
    ).astype(jnp.float32)
    returned = lax.all_to_all(
        own_rows.astype(jnp.bfloat16), "exp", split_axis=0, concat_axis=0, tiled=True
    ).astype(own_rows.dtype)
    summed = jnp.sum(returned.reshape(splits, EXPERTS * capacity, D), axis=0)
    weights = jnp.sum(matches.astype(jnp.float32) * gate_vals.astype(jnp.float32)[None], axis=2)
    expert_out = jnp.dot(weights.T, summed, precision=lax.Precision.HIGHEST)
    return (hidden_state + expert_out.reshape(hidden_state.shape)).astype(jnp.bfloat16)


def solution(mesh):
    placed = (
        P("seq", None, "exp"),
        P("seq", None, "exp"),
        P(None, "exp"),
        P("exp"),
        P("exp", None),
        P(None, "exp"),
        P("exp"),
        P(None, "exp"),
        P("exp"),
        P("exp", None),
        P(("seq", "exp"), None, None),
        P(),
        P(("seq", "exp"), None, None),
        P(("seq", "exp"), None, None),
        P("exp", None, "seq"),
        P("exp", None, "seq"),
        P("exp", "seq", None),
    )
    return jax.shard_map(
        per_device,
        mesh=mesh,
        in_specs=placed,
        out_specs=P(("seq", "exp"), None, None),
        check_vma=False,
    )
```

profile of v0, /device:TPU:2, one launch (start us, length us, event | category | flops | bytes accessed | tf_op | source)
XLA Modules:
  0.0 485.4 jit_solution(7767882943626385610)
XLA Ops:
  6.6 0.8 slice.38
  7.4 1.9 collective-permute-start
  9.3 0.9 fusion.43
  10.2 2.2 collective-permute-done
  12.4 1.1 maximum_convert_fusion
  13.5 1.2 fusion.39
  14.7 1.0 convolution_convert_fusion.3
  15.8 86.0 %all-reduce.4.cloned.1.call-done = bf16[64,4,288]{2,0,1:T(8,128)(2,1)} async-done(((bf16[64,4,288]{2,0,1:T(8,128)(2,1)}), bf16[64,4,288]{2,0,1:T(8,128)(2,1)}) %all-reduce.4.cloned.1.call-update) | async-done | bytes 147472 | tf_op jit(solution)/shard_map/psum | solution.py:102
  101.8 1.2 fusion.35
  103.6 1.7 fusion.42
  105.4 10.3 %while.37 = (s32[]{:T(128)}, f32[4,16,512]{2,1,0:T(8,128)S(1)}, f32[64,4,512]{2,1,0:T(4,128)S(1)}, f32[16,512]{1,0:T(8,128)S(1)}, f32[64,4,512]{2,1,0:T(4,128)S(...) while((s32[]{:T(128)}, f32[4,16,512]{2,1,0:T(8,128)S(1)}, f32[64,4,512]{2,1,0:T(4,128)S(1)}, ...), condition=%wide.region_3.4_spmd.clone, body=%wide.region_2.3_spmd.clone.sunk | while | flops 165891 | bytes 353131 | solution.py:114
  115.7 13.1 %all-gather = bf16[32,16,512]{2,1,0:T(8,128)(2,1)S(1)} all-gather(bf16[4,16,512]{2,1,0:T(8,128)(2,1)S(1)} %convert_element_type.103), channel_id=2, replica_groups=mesh['seq'=8,'exp'=16] {'seq'}, dimensions={0}, use_global_device_ids=true | all-gather | bytes 589824 | tf_op jit(solution)/shard_map/all_gather | solution.py:23
  128.9 13.1 %all_gather.13 = bf16[8,4,16,512]{3,2,1,0:T(8,128)(2,1)S(1)} all-gather(bf16[1,4,16,512]{3,2,1,0:T(8,128)(2,1)S(1)} %exponential_convert_fusion), channel_id=1, replica_groups=mesh['seq'=8,'exp'=16] {'seq'}, dimensions={0}, use_global_device_ids=true | all-gather | bytes 589824 | tf_op jit(solution)/shard_map/all_gather | solution.py:23
  142.2 58.7 %while.36 = (s32[]{:T(128)}, f32[4,16,512]{2,1,0:T(8,128)S(1)}, f32[64,4,512]{2,1,0:T(4,128)S(1)}, f32[64,4,512]{2,1,0:T(4,128)S(1)}, f32[16,512]{1,0:T(8,128)S(...) while((s32[]{:T(128)}, f32[4,16,512]{2,1,0:T(8,128)S(1)}, ...), condition=%wide.region_8.9_spmd, body=%wide.region_6.8_spmd.sunk | while | flops 196610 | bytes 378481 | solution.py:118
  142.2 0.7 constant_dynamic-slice_fusion.3
  143.1 0.7 constant_dynamic-slice_fusion.3
  144.1 0.7 constant_dynamic-slice_fusion.3
  145.0 0.7 constant_dynamic-slice_fusion.3
  178.8 0.8 constant_dynamic-slice_fusion.3
  179.7 0.8 constant_dynamic-slice_fusion.3
  180.7 0.8 constant_dynamic-slice_fusion.3
  181.6 0.8 constant_dynamic-slice_fusion.3
  182.5 0.8 constant_dynamic-slice_fusion.3
  183.5 0.8 constant_dynamic-slice_fusion.3
  184.4 0.8 constant_dynamic-slice_fusion.3
  185.4 0.8 constant_dynamic-slice_fusion.3
  193.6 0.7 constant_dynamic-slice_fusion.3
  194.5 0.7 constant_dynamic-slice_fusion.3
  195.4 0.7 constant_dynamic-slice_fusion.3
  196.4 0.7 constant_dynamic-slice_fusion.3
  197.3 0.7 constant_dynamic-slice_fusion.3
  198.2 0.7 constant_dynamic-slice_fusion.3
  199.1 0.7 constant_dynamic-slice_fusion.3
  200.0 0.7 constant_dynamic-slice_fusion.3
  200.9 1.3 fusion.30
  202.3 4.8 convolution_convert_fusion.1
  209.3 87.8 %all-reduce.6.cloned.1.call-done = bf16[64,4,4096]{2,0,1:T(8,128)(2,1)} async-done(((bf16[64,4,4096]{2,0,1:T(8,128)(2,1)}), bf16[64,4,4096]{2,0,1:T(8,128)(2,1)}) %all-reduce.6.cloned.1.call-update) | async-done | bytes 2097168
  297.1 1.0 constant_dynamic-slice_fusion.1
  299.1 20.6 %all_to_all.10 = bf16[16,8,4096]{2,1,0:T(8,128)(2,1)} all-to-all(bf16[16,8,4096]{2,1,0:T(8,128)(2,1)S(1)} %bitcast.113), channel_id=1, replica_groups=mesh['seq'=8,'exp'=16] {'exp'}, dimensions={0} | all-to-all | bytes 2097152 | tf_op jit(solution)/shard_map/all_to_all | solution.py:147
  319.9 46.7 %all-gather.3.cloned.1.call-done = bf16[128,8,4096]{2,1,0:T(8,128)(2,1)} async-done(((bf16[16,8,4096]{2,1,0:T(8,128)(2,1)}), bf16[128,8,4096]{2,1,0:T(8,128)(2,1)}) %all-gather.3.cloned.1.call-update) | async-done | bytes 8388624 | tf_op jit(solution)/shard_map/all_gather | solution.py:150
  366.6 11.0 %fusion.1 = f32[1024,768]{1,0:T(8,128)S(1)} fusion(bf16[128,8,4096]{2,1,0:T(8,128)(2,1)} %all-gather.3.cloned.1.call-done, bf16[1,4096,768]{2,1,0:T(8,128)(2,1)} %param.38), kind=kOutput, calls=%fused_computation.14 | convolution fusion | flops 6442450944 | bytes 17825792 | tf_op jit(solution)/shard_map/dot_general | solution.py:154
  377.7 9.9 %fusion.16 = bf16[128,8,768]{2,1,0:T(8,128)(2,1)S(1)} fusion(f32[1024,768]{1,0:T(8,128)S(1)} %fusion.1, bf16[1,4096,768]{2,1,0:T(8,128)(2,1)} %param.37, bf16[128,8,4096]{2,1,0:T(8,128)(2,1)S(1)} %copy-done.9), kind=kOutput, calls=%fused_computation.31 | convolution fusion | flops 6447169536 | bytes 19398656 | tf_op jit(solution)/shard_map/dot_general | solution.py:153
  387.6 8.9 %convolution_convert_fusion = bf16[128,8,4096]{2,0,1:T(8,128)(2,1)} fusion(bf16[1,768,4096]{2,1,0:T(8,128)(2,1)S(1)} %bitcast.122, bf16[128,8,768]{2,1,0:T(8,128)(2,1)S(1)} %fusion.16), kind=kOutput, calls=%fused_computation.18 | convolution fusion | flops 6446645248 | bytes 16252928 | tf_op jit(solution)/shard_map/dot_general | solution.py:157
  396.5 51.1 %reduce-scatter.3.cloned.1.call-done = bf16[16,8,4096]{2,0,1:T(8,128)(2,1)} async-done(((bf16[128,8,4096]{2,0,1:T(8,128)(2,1)}), bf16[16,8,4096]{2,0,1:T(8,128)(2,1)}) %reduce-scatter.3.cloned.1.call-update) | async-done | bytes 1048592 | tf_op jit(solution)/shard_map/reduce_scatter | solution.py:156
  447.7 2.8 copy.87
  450.4 7.2 %all-to-all-start.1 = ((bf16[16,8,4096]{2,1,0:T(8,128)(2,1)}), bf16[16,8,4096]{2,1,0:T(8,128)(2,1)S(1)}, u32[]{:S(2)}, u32[]{:S(2)}) async-start(bf16[16,8,4096]{2,1,0:T(8,128)(2,1)} %copy.87), calls=%async_computation.2 | async-start | bytes 2097152 | tf_op jit(solution)/shard_map/all_to_all | solution.py:164
  457.9 19.5 %all-to-all-done.1 = bf16[16,8,4096]{2,1,0:T(8,128)(2,1)S(1)} async-done(((bf16[16,8,4096]{2,1,0:T(8,128)(2,1)}), bf16[16,8,4096]{2,1,0:T(8,128)(2,1)S(1)}, u32[]{:S(2)}, u32[]{:S(2)}) %all-to-all-start.1) | async-done | bytes 1048608 | tf_op jit(solution)/shard_map/all_to_all | solution.py:164
  477.5 1.4 fusion.9
  (690 shorter events, 53.2 us)
Async XLA Ops:
  6.5 8.1 %copy-start = (bf16[512,288]{0,1:T(8,128)(2,1)S(1)}, bf16[512,288]{0,1:T(8,128)(2,1)}, u32[]{:S(2)}) copy-start(bf16[512,288]{0,1:T(8,128)(2,1)} %param.27) | copy-start | bytes 884740
  6.5 9.2 %copy-start.3 = (f32[16,512]{1,0:T(8,128)S(1)}, f32[16,512]{1,0:T(8,128)}, u32[]{:S(2)}) copy-start(f32[16,512]{1,0:T(8,128)} %param.30) | copy-start | bytes 98308
  6.5 95.3 %copy-start.2 = (bf16[256,512]{1,0:T(8,128)(2,1)S(1)}, bf16[256,512]{1,0:T(8,128)(2,1)}, u32[]{:S(2)}) copy-start(bf16[256,512]{1,0:T(8,128)(2,1)} %param.28) | copy-start | bytes 786436
  6.5 95.3 %copy-start.6 = (f32[512]{0:T(512)S(1)}, f32[512]{0:T(512)}, u32[]{:S(2)}) copy-start(f32[512]{0:T(512)} %param.29) | copy-start | bytes 6148
  6.5 95.2 %all-reduce.4.cloned.1.call-start = ((), (), s32[]{:S(2)}) async-start(), calls=%async_computation.3 | async-start | bytes 393216 | tf_op jit(solution)/shard_map/psum | solution.py:102
  7.4 5.0 %collective-permute-start = (bf16[3,4,512]{2,1,0:T(4,128)(2,1)S(1)}, bf16[3,4,512]{2,1,0:T(4,128)(2,1)S(1)}, u32[]{:S(2)}, u32[]{:S(2)}) collective-permute-start(bf16[3,4,512]{2,1,0:T(4,128)(2,1)S(1)} %slice.38), channel_id=1, source_target_pairs={{0,16},{16,32},{32,48},{48,64},{64,80},{80,96},{96,112},{1,17},{17... | collective-permute-start | bytes 36872 | tf_op jit(solution)/shard_map/ppermute | solution.py:17
  15.7 281.4 %all-reduce.6.cloned.1.call-start = ((), (), s32[]{:S(2)}) async-start(), calls=%async_computation.6 | async-start | bytes 4194304
  105.3 95.6 %copy-start.7 = (f32[512]{0:T(512)S(1)}, f32[512]{0:T(512)}, u32[]{:S(2)}) copy-start(f32[512]{0:T(512)} %param.31) | copy-start | bytes 6148
  202.3 4.9 %copy-start.5 = (s32[4,4,2]{1,2,0:T(2,128)S(1)}, s32[4,4,2]{1,2,0:T(2,128)}, u32[]{:S(2)}) copy-start(s32[4,4,2]{1,2,0:T(2,128)} %param.35) | copy-start | bytes 388
  202.3 5.7 %copy-start.10 = (u32[128]{0:T(128)S(1)}, u32[128]{0:T(128)}, u32[]{:S(2)}) copy-start(u32[128]{0:T(128)} %constant.77) | copy-start | bytes 1540
  202.3 95.9 %copy-start.1 = (bf16[4,4,4096]{2,1,0:T(4,128)(2,1)S(1)}, bf16[4,4,4096]{2,1,0:T(4,128)(2,1)}, u32[]{:S(2)}) copy-start(bf16[4,4,4096]{2,1,0:T(4,128)(2,1)} %param.33) | copy-start | bytes 393220
  202.3 96.1 %copy-start.4 = (f32[4096]{0:T(1024)S(1)}, f32[4096]{0:T(1024)}, u32[]{:S(2)}) copy-start(f32[4096]{0:T(1024)} %param.34) | copy-start | bytes 49156
  207.1 159.5 %all-gather.3.cloned.1.call-start = ((), (), s32[]{:S(2)}) async-start(), calls=%async_computation.4 | async-start | bytes 9437184 | tf_op jit(solution)/shard_map/all_gather | solution.py:150
  319.7 128.0 %reduce-scatter.3.cloned.1.call-start = ((), (), s32[]{:S(2)}) async-start(), calls=%async_computation.5 | async-start | bytes 9437184 | tf_op jit(solution)/shard_map/reduce_scatter | solution.py:156
  366.6 11.0 %copy-start.9 = (bf16[128,8,4096]{2,1,0:T(8,128)(2,1)S(1)}, bf16[128,8,4096]{2,1,0:T(8,128)(2,1)}, u32[]{:S(2)}) copy-start(bf16[128,8,4096]{2,1,0:T(8,128)(2,1)} %all-gather.3.cloned.1.call-done) | copy-start | bytes 25165828
  366.6 21.0 %slice-start = ((s8[6291456]{0:T(1024)(128)(4,1)}), s8[4194304]{0:T(1024)(128)(4,1)S(1)}, s32[]{:S(2)}) async-start(s8[6291456]{0:T(1024)(128)(4,1)} %bitcast.121), calls=%async_computation.7 | async-start | bytes 8388608
  377.7 10.0 %slice-start.1 = ((s8[6291456]{0:T(1024)(128)(4,1)}), s8[2097152]{0:T(1024)(128)(4,1)S(1)}, s32[]{:S(2)}) async-start(s8[6291456]{0:T(1024)(128)(4,1)} %bitcast.121), calls=%async_computation.8 | async-start | bytes 4194304
  396.5 61.2 %copy-start.8 = (bf16[4,4,2]{1,2,0:T(2,128)(2,1)S(1)}, bf16[4,4,2]{1,2,0:T(2,128)(2,1)}, u32[]{:S(2)}) copy-start(bf16[4,4,2]{1,2,0:T(2,128)(2,1)} %param.36) | copy-start | bytes 196
  450.4 26.9 %all-to-all-start.1 = ((bf16[16,8,4096]{2,1,0:T(8,128)(2,1)}), bf16[16,8,4096]{2,1,0:T(8,128)(2,1)S(1)}, u32[]{:S(2)}, u32[]{:S(2)}) async-start(bf16[16,8,4096]{2,1,0:T(8,128)(2,1)} %copy.87), calls=%async_computation.2 | async-start | bytes 2097152 | tf_op jit(solution)/shard_map/all_to_all | solution.py:164
Sparse Core Ops, SparseCore 0:
  15.8 85.9 all-reduce.3
  207.3 89.8 all-reduce.5
  319.8 46.7 all-gather.2
  396.7 50.9 reduce-scatter.2
where the time goes:
time: 489 us; the launch traced here: 485 us
  waiting for transfers between devices  293 us (60%)
  local copies, waits for them, and re-layouts  58.7 us (12%)
  blocking collectives  46.9 us (10%)
  matrix products  38.5 us (8%)
  other arithmetic  19.2 us (4%)
  between operations  14.1 us (3%)
  starting transfers between devices  9.47 us (2%)
  loops' own time  5.32 us (1%)
    unnamed x5, waiting for transfers between devices  87.8 us
    psum x1, waiting for transfers between devices, per_device(): lax.psum(projected.astype(jnp.bfloat16), 'exp').astype(jnp.float32)  86 us
    reduce_scatter x1, waiting for transfers between devices, per_device(): lax.psum_scatter(jnp.dot(hidden, w_down[0], preferred_element_type=jnp.fl...  51.1 us
    dynamic_slice x64, local copies, waits for them, and re-layouts, per_device(): final_local, local_out = lax.scan(advance, zero_state, series)  47 us
    all_gather x1, waiting for transfers between devices, per_device(): everything = lax.all_gather(arrived, 'seq', axis=0, tiled=True)  46.7 us
    all_gather x2, blocking collectives, entering(): lax.all_gather(a.astype(kind), axis)  26.2 us
    all_to_all x1, blocking collectives, per_device(): lax.all_to_all(jnp.tile(outgoing, (splits, 1, 1)), 'exp', split_axis=0, c...  20.6 us
    all_to_all x1, waiting for transfers between devices, per_device(): lax.all_to_all(own_rows.astype(jnp.bfloat16), 'exp', split_axis=0, concat...  19.5 us
  transfers between devices with their start and end apart: 6, of which 6 were waited for; matrix products, arithmetic and copies ran while one was open for 1% of the time, Pallas kernels for 0%

commit v1 on v0

--- a/solution.py
+++ b/solution.py
@@ -99,7 +99,9 @@
     projected = jnp.einsum(
         "pbc,cr->pbr", inner_act, xproj_weight, preferred_element_type=jnp.float32
     )
-    projected = lax.psum(projected.astype(jnp.bfloat16), "exp").astype(jnp.float32)
+    projected = jnp.sum(lax.all_gather(projected.astype(jnp.bfloat16), "exp"), axis=0).astype(
+        jnp.float32
+    )
     low_rank = projected[..., :RANK].astype(jnp.bfloat16)
     in_state = projected[..., RANK : RANK + STATE]
     out_state = projected[..., RANK + STATE :]

time: 489 us -> 454 us (0.928)
  waiting for transfers between devices: 293 us -> 257 us
    psum x1 -> x0, waiting for transfers between devices: 86 us -> none  [per_device(): lax.psum(projected.astype(jnp.bfloat16), 'exp').astype(jnp.float32)]
    all_gather x0 -> x1, waiting for transfers between devices: none -> 50.5 us  [per_device(): lax.all_gather(projected.astype(jnp.bfloat16), 'exp')]
where the time goes in v1:
time: 454 us; the launch traced here: 450 us
  waiting for transfers between devices  257 us (57%)
  local copies, waits for them, and re-layouts  57.8 us (13%)
  blocking collectives  46.9 us (10%)
  matrix products  37.6 us (8%)
  other arithmetic  21.6 us (5%)
  between operations  14.1 us (3%)
  starting transfers between devices  9.42 us (2%)
  loops' own time  5.32 us (1%)
    unnamed x5, waiting for transfers between devices  87.3 us
    reduce_scatter x1, waiting for transfers between devices, per_device(): lax.psum_scatter(jnp.dot(hidden, w_down[0], preferred_element_type=jnp.fl...  51.1 us
    all_gather x1, waiting for transfers between devices, per_device(): lax.all_gather(projected.astype(jnp.bfloat16), 'exp')  50.5 us
    dynamic_slice x64, local copies, waits for them, and re-layouts, per_device(): final_local, local_out = lax.scan(advance, zero_state, series)  47 us
    all_gather x1, waiting for transfers between devices, per_device(): everything = lax.all_gather(arrived, 'seq', axis=0, tiled=True)  46.6 us
    all_gather x2, blocking collectives, entering(): lax.all_gather(a.astype(kind), axis)  26.2 us
    all_to_all x1, blocking collectives, per_device(): lax.all_to_all(jnp.tile(outgoing, (splits, 1, 1)), 'exp', split_axis=0, c...  20.6 us
    all_to_all x1, waiting for transfers between devices, per_device(): lax.all_to_all(own_rows.astype(jnp.bfloat16), 'exp', split_axis=0, concat...  19.4 us
  transfers between devices with their start and end apart: 6, of which 6 were waited for; matrix products, arithmetic and copies ran while one was open for 1% of the time, Pallas kernels for 0%

profile of v1, /device:TPU:2, one launch (start us, length us, event | category | flops | bytes accessed | tf_op | source)
XLA Modules:
  0.0 450.0 jit_solution(5745010577629147568)
XLA Ops:
  6.5 0.8 slice.38
  7.3 1.9 collective-permute-start
  9.2 0.9 fusion.43
  10.1 2.2 collective-permute-done
  12.3 1.1 maximum_convert_fusion
  13.4 1.2 fusion.39
  14.6 1.0 convolution_convert_fusion.3
  15.7 50.5 %all-gather.7.cloned.1.call-done = bf16[1024,4,288]{2,0,1:T(8,128)(2,1)} async-done(((bf16[64,4,288]{2,0,1:T(8,128)(2,1)}), bf16[1024,4,288]{2,0,1:T(8,128)(2,1)}) %all-gather.7.cloned.1.call-update) | async-done | bytes 2359312 | tf_op jit(solution)/shard_map/all_gather | solution.py:102
  66.3 2.5 reduce_sum.77
  68.8 0.7 fusion.42
  70.6 10.3 %while.37 = (s32[]{:T(128)}, f32[4,16,512]{2,1,0:T(8,128)S(1)}, f32[64,4,512]{2,1,0:T(4,128)S(1)}, f32[16,512]{1,0:T(8,128)S(1)}, f32[64,4,512]{2,1,0:T(4,128)S(...) while((s32[]{:T(128)}, f32[4,16,512]{2,1,0:T(8,128)S(1)}, f32[64,4,512]{2,1,0:T(4,128)S(1)}, ...), condition=%wide.region_3.4_spmd.clone, body=%wide.region_2.3_spmd.clone.sunk | while | flops 165891 | bytes 353131 | solution.py:116
  80.9 13.1 %all-gather.1 = bf16[32,16,512]{2,1,0:T(8,128)(2,1)S(1)} all-gather(bf16[4,16,512]{2,1,0:T(8,128)(2,1)S(1)} %convert_element_type.105), channel_id=3, replica_groups=mesh['seq'=8,'exp'=16] {'seq'}, dimensions={0}, use_global_device_ids=true | all-gather | bytes 589824 | tf_op jit(solution)/shard_map/all_gather | solution.py:23
  94.0 13.1 %all_gather.21 = bf16[8,4,16,512]{3,2,1,0:T(8,128)(2,1)S(1)} all-gather(bf16[1,4,16,512]{3,2,1,0:T(8,128)(2,1)S(1)} %exponential_convert_fusion), channel_id=1, replica_groups=mesh['seq'=8,'exp'=16] {'seq'}, dimensions={0}, use_global_device_ids=true | all-gather | bytes 589824 | tf_op jit(solution)/shard_map/all_gather | solution.py:23
  107.3 58.7 %while.36 = (s32[]{:T(128)}, f32[4,16,512]{2,1,0:T(8,128)S(1)}, f32[64,4,512]{2,1,0:T(4,128)S(1)}, f32[64,4,512]{2,1,0:T(4,128)S(1)}, f32[16,512]{1,0:T(8,128)S(...) while((s32[]{:T(128)}, f32[4,16,512]{2,1,0:T(8,128)S(1)}, ...), condition=%wide.region_8.9_spmd, body=%wide.region_6.8_spmd.sunk | while | flops 196610 | bytes 378481 | solution.py:120
  107.4 0.7 constant_dynamic-slice_fusion.3
  108.3 0.7 constant_dynamic-slice_fusion.3
  112.0 0.7 constant_dynamic-slice_fusion.3
  113.8 0.7 constant_dynamic-slice_fusion.3
  144.0 0.8 constant_dynamic-slice_fusion.3
  144.9 0.8 constant_dynamic-slice_fusion.3
  145.8 0.8 constant_dynamic-slice_fusion.3
  146.8 0.8 constant_dynamic-slice_fusion.3
  147.7 0.8 constant_dynamic-slice_fusion.3
  148.6 0.8 constant_dynamic-slice_fusion.3
  149.6 0.8 constant_dynamic-slice_fusion.3
  150.5 0.8 constant_dynamic-slice_fusion.3
  158.8 0.7 constant_dynamic-slice_fusion.3
  159.7 0.7 constant_dynamic-slice_fusion.3
  160.6 0.7 constant_dynamic-slice_fusion.3
  161.5 0.7 constant_dynamic-slice_fusion.3
  162.4 0.7 constant_dynamic-slice_fusion.3
  163.4 0.7 constant_dynamic-slice_fusion.3
  164.3 0.7 constant_dynamic-slice_fusion.3
  165.2 0.7 constant_dynamic-slice_fusion.3
  166.1 1.3 fusion.30
  167.5 4.8 %convolution_convert_fusion.1 = bf16[64,4,4096]{2,0,1:T(8,128)(2,1)} fusion(bf16[512,4096]{1,0:T(8,128)(2,1)} %param.32, bf16[64,4,512]{2,1,0:T(4,128)(2,1)S(1)} %fusion.30), kind=kOutput, calls=%fused_computation.22 | convolution fusion | flops 1074790400 | bytes 6553600 | tf_op jit(solution)/shard_map/pbc,cd->pbd/dot_general | solution.py:126
  174.5 87.2 %all-reduce.3.cloned.1.call-done = bf16[64,4,4096]{2,0,1:T(8,128)(2,1)} async-done(((bf16[64,4,4096]{2,0,1:T(8,128)(2,1)}), bf16[64,4,4096]{2,0,1:T(8,128)(2,1)}) %all-reduce.3.cloned.1.call-update) | async-done | bytes 2097168
  261.7 1.0 constant_dynamic-slice_fusion.1
  263.7 20.6 %all_to_all.10 = bf16[16,8,4096]{2,1,0:T(8,128)(2,1)} all-to-all(bf16[16,8,4096]{2,1,0:T(8,128)(2,1)S(1)} %bitcast.114), channel_id=1, replica_groups=mesh['seq'=8,'exp'=16] {'exp'}, dimensions={0} | all-to-all | bytes 2097152 | tf_op jit(solution)/shard_map/all_to_all | solution.py:149
  284.6 46.6 %all-gather.5.cloned.1.call-done = bf16[128,8,4096]{2,1,0:T(8,128)(2,1)} async-done(((bf16[16,8,4096]{2,1,0:T(8,128)(2,1)}), bf16[128,8,4096]{2,1,0:T(8,128)(2,1)}) %all-gather.5.cloned.1.call-update) | async-done | bytes 8388624 | tf_op jit(solution)/shard_map/all_gather | solution.py:152
  331.2 11.0 %fusion.1 = f32[1024,768]{1,0:T(8,128)S(1)} fusion(bf16[128,8,4096]{2,1,0:T(8,128)(2,1)} %all-gather.5.cloned.1.call-done, bf16[1,4096,768]{2,1,0:T(8,128)(2,1)} %param.38), kind=kOutput, calls=%fused_computation.14 | convolution fusion | flops 6442450944 | bytes 17825792 | tf_op jit(solution)/shard_map/dot_general | solution.py:156
  342.3 9.9 %fusion.16 = bf16[128,8,768]{2,1,0:T(8,128)(2,1)S(1)} fusion(f32[1024,768]{1,0:T(8,128)S(1)} %fusion.1, bf16[1,4096,768]{2,1,0:T(8,128)(2,1)} %param.37, bf16[128,8,4096]{2,1,0:T(8,128)(2,1)S(1)} %copy-done.9), kind=kOutput, calls=%fused_computation.31 | convolution fusion | flops 6447169536 | bytes 19398656 | tf_op jit(solution)/shard_map/dot_general | solution.py:155
  352.3 8.9 %convolution_convert_fusion = bf16[128,8,4096]{2,0,1:T(8,128)(2,1)} fusion(bf16[1,768,4096]{2,1,0:T(8,128)(2,1)S(1)} %bitcast.124, bf16[128,8,768]{2,1,0:T(8,128)(2,1)S(1)} %fusion.16), kind=kOutput, calls=%fused_computation.18 | convolution fusion | flops 6446645248 | bytes 16252928 | tf_op jit(solution)/shard_map/dot_general | solution.py:159
  361.2 51.1 %reduce-scatter.3.cloned.1.call-done = bf16[16,8,4096]{2,0,1:T(8,128)(2,1)} async-done(((bf16[128,8,4096]{2,0,1:T(8,128)(2,1)}), bf16[16,8,4096]{2,0,1:T(8,128)(2,1)}) %reduce-scatter.3.cloned.1.call-update) | async-done | bytes 1048592 | tf_op jit(solution)/shard_map/reduce_scatter | solution.py:158
  412.3 2.8 copy.87
  415.1 7.2 %all-to-all-start.1 = ((bf16[16,8,4096]{2,1,0:T(8,128)(2,1)}), bf16[16,8,4096]{2,1,0:T(8,128)(2,1)S(1)}, u32[]{:S(2)}, u32[]{:S(2)}) async-start(bf16[16,8,4096]{2,1,0:T(8,128)(2,1)} %copy.87), calls=%async_computation.2 | async-start | bytes 2097152 | tf_op jit(solution)/shard_map/all_to_all | solution.py:166
  422.5 19.4 %all-to-all-done.1 = bf16[16,8,4096]{2,1,0:T(8,128)(2,1)S(1)} async-done(((bf16[16,8,4096]{2,1,0:T(8,128)(2,1)}), bf16[16,8,4096]{2,1,0:T(8,128)(2,1)S(1)}, u32[]{:S(2)}, u32[]{:S(2)}) %all-to-all-start.1) | async-done | bytes 1048608 | tf_op jit(solution)/shard_map/all_to_all | solution.py:166
  442.1 1.4 fusion.9
  (691 shorter events, 53.4 us)
Async XLA Ops:
  6.5 8.1 %copy-start = (bf16[512,288]{0,1:T(8,128)(2,1)S(1)}, bf16[512,288]{0,1:T(8,128)(2,1)}, u32[]{:S(2)}) copy-start(bf16[512,288]{0,1:T(8,128)(2,1)} %param.27) | copy-start | bytes 884740
  6.5 9.2 %copy-start.3 = (f32[16,512]{1,0:T(8,128)S(1)}, f32[16,512]{1,0:T(8,128)}, u32[]{:S(2)}) copy-start(f32[16,512]{1,0:T(8,128)} %param.30) | copy-start | bytes 98308
  6.5 59.7 %all-gather.7.cloned.1.call-start = ((), (), s32[]{:S(2)}) async-start(), calls=%async_computation.5 | async-start | bytes 3342336 | tf_op jit(solution)/shard_map/all_gather | solution.py:102
  7.3 5.0 %collective-permute-start = (bf16[3,4,512]{2,1,0:T(4,128)(2,1)S(1)}, bf16[3,4,512]{2,1,0:T(4,128)(2,1)S(1)}, u32[]{:S(2)}, u32[]{:S(2)}) collective-permute-start(bf16[3,4,512]{2,1,0:T(4,128)(2,1)S(1)} %slice.38), channel_id=1, source_target_pairs={{0,16},{16,32},{32,48},{48,64},{64,80},{80,96},{96,112},{1,17},{17... | collective-permute-start | bytes 36872 | tf_op jit(solution)/shard_map/ppermute | solution.py:17
  10.1 59.4 %copy-start.2 = (bf16[256,512]{1,0:T(8,128)(2,1)S(1)}, bf16[256,512]{1,0:T(8,128)(2,1)}, u32[]{:S(2)}) copy-start(bf16[256,512]{1,0:T(8,128)(2,1)} %param.28) | copy-start | bytes 786436
  10.1 59.4 %copy-start.6 = (f32[512]{0:T(512)S(1)}, f32[512]{0:T(512)}, u32[]{:S(2)}) copy-start(f32[512]{0:T(512)} %param.29) | copy-start | bytes 6148
  15.6 246.1 %all-reduce.3.cloned.1.call-start = ((), (), s32[]{:S(2)}) async-start(), calls=%async_computation.6 | async-start | bytes 4194304
  70.5 95.6 %copy-start.7 = (f32[512]{0:T(512)S(1)}, f32[512]{0:T(512)}, u32[]{:S(2)}) copy-start(f32[512]{0:T(512)} %param.31) | copy-start | bytes 6148
  167.4 4.9 %copy-start.5 = (s32[4,4,2]{1,2,0:T(2,128)S(1)}, s32[4,4,2]{1,2,0:T(2,128)}, u32[]{:S(2)}) copy-start(s32[4,4,2]{1,2,0:T(2,128)} %param.35) | copy-start | bytes 388
  167.4 5.7 %copy-start.10 = (u32[128]{0:T(128)S(1)}, u32[128]{0:T(128)}, u32[]{:S(2)}) copy-start(u32[128]{0:T(128)} %constant.79) | copy-start | bytes 1540
  167.4 95.3 %copy-start.1 = (bf16[4,4,4096]{2,1,0:T(4,128)(2,1)S(1)}, bf16[4,4,4096]{2,1,0:T(4,128)(2,1)}, u32[]{:S(2)}) copy-start(bf16[4,4,4096]{2,1,0:T(4,128)(2,1)} %param.33) | copy-start | bytes 393220
  167.5 95.6 %copy-start.4 = (f32[4096]{0:T(1024)S(1)}, f32[4096]{0:T(1024)}, u32[]{:S(2)}) copy-start(f32[4096]{0:T(1024)} %param.34) | copy-start | bytes 49156
  172.3 158.9 %all-gather.5.cloned.1.call-start = ((), (), s32[]{:S(2)}) async-start(), calls=%async_computation.3 | async-start | bytes 9437184 | tf_op jit(solution)/shard_map/all_gather | solution.py:152
  284.3 127.9 %reduce-scatter.3.cloned.1.call-start = ((), (), s32[]{:S(2)}) async-start(), calls=%async_computation.4 | async-start | bytes 9437184 | tf_op jit(solution)/shard_map/reduce_scatter | solution.py:158
  331.2 11.1 %copy-start.9 = (bf16[128,8,4096]{2,1,0:T(8,128)(2,1)S(1)}, bf16[128,8,4096]{2,1,0:T(8,128)(2,1)}, u32[]{:S(2)}) copy-start(bf16[128,8,4096]{2,1,0:T(8,128)(2,1)} %all-gather.5.cloned.1.call-done) | copy-start | bytes 25165828
  331.2 21.0 %slice-start = ((s8[6291456]{0:T(1024)(128)(4,1)}), s8[4194304]{0:T(1024)(128)(4,1)S(1)}, s32[]{:S(2)}) async-start(s8[6291456]{0:T(1024)(128)(4,1)} %bitcast.123), calls=%async_computation.7 | async-start | bytes 8388608
  342.3 10.0 %slice-start.1 = ((s8[6291456]{0:T(1024)(128)(4,1)}), s8[2097152]{0:T(1024)(128)(4,1)S(1)}, s32[]{:S(2)}) async-start(s8[6291456]{0:T(1024)(128)(4,1)} %bitcast.123), calls=%async_computation.8 | async-start | bytes 4194304
  361.2 61.1 %copy-start.8 = (bf16[4,4,2]{1,2,0:T(2,128)(2,1)S(1)}, bf16[4,4,2]{1,2,0:T(2,128)(2,1)}, u32[]{:S(2)}) copy-start(bf16[4,4,2]{1,2,0:T(2,128)(2,1)} %param.36) | copy-start | bytes 196
  415.1 26.8 %all-to-all-start.1 = ((bf16[16,8,4096]{2,1,0:T(8,128)(2,1)}), bf16[16,8,4096]{2,1,0:T(8,128)(2,1)S(1)}, u32[]{:S(2)}, u32[]{:S(2)}) async-start(bf16[16,8,4096]{2,1,0:T(8,128)(2,1)} %copy.87), calls=%async_computation.2 | async-start | bytes 2097152 | tf_op jit(solution)/shard_map/all_to_all | solution.py:166
Sparse Core Ops, SparseCore 0:
  15.8 50.4 all-gather.6
  172.4 89.2 all-reduce.2
  284.5 46.7 all-gather.4
  361.3 50.9 reduce-scatter.2
